TPU v7x, 512 devices: a whole 4x4x16 slice. The times are simulated.
512 devices in a mesh: frames: 8 (over z_lo), slabs: 64 (over y, x, z_hi, core).
Axes of the slice: x: 4, y: 4, z: 16 (z_hi: 2, z_lo: 8; z = z_hi * 8 + z_lo), core: 2. Of those that a mesh axis runs over, the one named last changes fastest.
Arguments:
- movie: bfloat16 [64, 131072], P('frames', 'slabs'), may hold values from -48 to 48
- traces: bfloat16 [64, 1024], P('frames', 'slabs'), may hold values from -6 to 6
- voxel_index: int32 [1024, 2048], P('slabs'), may hold values from 0 to 4095, as said below
- footprint: float32 [1024, 2048], P('slabs'), may hold values from 0 to 1
- block_order: int32 [2], replicated, may hold values from 0 to 1, each once
Outputs:
- updated: float32 [1024, 2048], P('slabs')
Inputs may be any that keep to these rules, and one draw needn't show every extreme that they name: `voxel_index`: within a row all 2048 positions are distinct and lie in a run of 4096 consecutive positions, whose first and last position are both in the row.
All inputs are finite; a program needn't handle non-finite values.
Results may differ from a plain program's by a relative error of at most 0.0003.
Values may be sent and summed in bfloat16 or wider, within the bound.
No kernel may reach another device: no remote copies, remote signals or barrier semaphores. Data moves between devices by JAX's collectives and lax.ppermute only.
A program may use at most 64 MiB of HBM per device.

v0:
```python
import jax
import jax.numpy as jnp
from jax import lax
from jax.sharding import PartitionSpec as P

BLOCK_SIZE = 8
SWEEPS = 2


def padded(block, sides, width):
    for axis, dim in sides:
        count = lax.axis_size(axis)
        forward = [(i, i + 1) for i in range(count - 1)]
        backward = [(target, source) for source, target in forward]
        low = lax.ppermute(
            lax.slice_in_dim(block, block.shape[dim] - width, None, axis=dim), axis, forward
        )
        high = lax.ppermute(lax.slice_in_dim(block, 0, width, axis=dim), axis, backward)
        block = jnp.concatenate([low, block, high], axis=dim)
    return block


def shifted(value, axis, steps):
    count = lax.axis_size(axis)
    leading, last = (max(0, -steps), min(count, count - steps))
    return lax.ppermute(value, axis, [(source, source + steps) for source in range(leading, last)])


def transposed(left, right):
    return lax.dot_general(
        left, right, (((0,), (0,)), ((), ())), preferred_element_type=jnp.float32
    )


def product(left, right):
    return jnp.dot(left, right, precision=lax.Precision.HIGHEST, preferred_element_type=jnp.float32)


def pull_halves(g_rows, state, from_left, from_right):
    source_dev = state.shape[0]
    half = from_left.shape[1]
    g_left = g_rows[:, :source_dev]
    g_mid = g_rows[:, source_dev : 2 * source_dev]
    g_right = g_rows[:, 2 * source_dev :]
    first = product(g_left, from_left) + product(g_mid, state[:, :half])
    second = product(g_mid, state[:, half:]) + product(g_right, from_right)
    return jnp.concatenate([first, second], axis=1)


def sweep_blocks(current, left_rows, right_rows, stat, gram, support, block_order, puller):
    source_dev = current.shape[0]
    diagonal = jnp.diagonal(gram[:, source_dev : 2 * source_dev]) + 1.0

    def one_block(state, blk):
        start = blk * BLOCK_SIZE
        g_rows = lax.dynamic_slice_in_dim(gram, start, BLOCK_SIZE, 0)
        pulled = puller(g_rows, state, left_rows, right_rows)
        old = lax.dynamic_slice_in_dim(state, start, BLOCK_SIZE, 0)
        stat_rows = lax.dynamic_slice_in_dim(stat, start, BLOCK_SIZE, 0)
        mask_rows = lax.dynamic_slice_in_dim(support, start, BLOCK_SIZE, 0)
        scale = lax.dynamic_slice_in_dim(diagonal, start, BLOCK_SIZE, 0)
        fresh = mask_rows * jnp.maximum(old + (stat_rows - pulled) / scale[:, None], 0.0)
        return (lax.dynamic_update_slice_in_dim(state, fresh, start, 0), None)

    result, unused = lax.scan(one_block, current, block_order)
    return result


def local(movie, traces, voxel_index, footprint, block_order):
    voxel_dev = movie.shape[1]
    source_dev = traces.shape[1]
    extent = 2 * voxel_dev
    extended = padded(movie, (("slabs", 1),), voxel_dev // 2)
    nearby = padded(traces, (("slabs", 1),), source_dev)
    stat_part = transposed(traces, extended)
    gram_part = transposed(traces, nearby)
    rows = jnp.arange(source_dev)[:, None]
    dense = jnp.zeros((source_dev, extent), jnp.float32).at[rows, voxel_index].set(footprint)
    support = jnp.zeros((source_dev, extent), jnp.float32).at[rows, voxel_index].set(1.0)
    stat, gram = lax.psum((stat_part, gram_part), "frames")
    for sweep in range(SWEEPS):
        from_left = shifted(dense[:, voxel_dev:], "slabs", 1)
        from_right = shifted(dense[:, :voxel_dev], "slabs", -1)
        dense = sweep_blocks(
            dense, from_left, from_right, stat, gram, support, block_order, pull_halves
        )
    return dense[rows, voxel_index]


def solution(mesh):
    in_specs = (P("frames", "slabs"), P("frames", "slabs"), P("slabs", None), P("slabs", None), P())
    out_specs = P("slabs", None)
    return jax.shard_map(local, mesh=mesh, in_specs=in_specs, out_specs=out_specs, check_vma=False)
```

profile of v0, /device:TPU:1, one launch (start us, length us, event | category | flops | bytes accessed | tf_op | source)
XLA Modules:
  0.0 709.6 jit_solution(1828707508935815415)
XLA Ops:
  6.5 17.0 %collective-permute-start.2 = (bf16[8,16]{1,0:T(8,128)(2,1)}, bf16[8,16]{1,0:T(8,128)(2,1)S(1)}, u32[]{:S(2)}, u32[]{:S(2)}) collective-permute-start(bf16[8,16]{1,0:T(8,128)(2,1)} %param.10), channel_id=1, source_target_pairs={{0,1},{1,2},{2,3},{3,4},{4,5},{5,6},{6,7},{7,8},{8,9},{9,10},{10,1... | collective-permute-start | bytes 776 | tf_op jit(solution)/shard_map/ppermute | solution.py:15
  23.5 1.9 collective-permute-start.3
  25.4 0.9 fusion.26
  26.5 0.5 copy-done.7
  27.2 0.8 copy-done.4
  28.1 120.1 %scatter_custom_fusion = f32[65536]{0:T(1024)S(1)} fusion(s32[32768]{0:T(1024)S(1)} %bitcast.41, f32[32768]{0:T(1024)S(1)} %bitcast.43, f32[]{:T(128)} %constant.34.clone.1), kind=kCustom, calls=%fused_computation.48 | custom fusion | bytes 262148
  148.3 12.4 %collective-permute-start.4 = (f32[16,2048]{1,0:T(8,128)S(1)}, f32[16,2048]{1,0:T(8,128)S(1)}, u32[]{:S(2)}, u32[]{:S(2)}) collective-permute-start(f32[16,2048]{1,0:T(8,128)S(1)} %get-tuple-element.140), channel_id=1, source_target_pairs={{0,1},{1,2},{2,3},{3,4},{4,5},{5,6},{6,7},{7,8},{8,9},{9,10},{10,1... | collective-permute-start | bytes 393224 | tf_op jit(solution)/shard_map/ppermute | solution.py:26
  160.7 1.9 collective-permute-start
  162.6 2.4 collective-permute-start.1
  165.1 120.1 %scatter_custom_fusion.1 = f32[65536]{0:T(1024)S(1)} fusion(s32[32768]{0:T(1024)S(1)} %bitcast.42, f32[32768]{0:T(1024)S(1)} %broadcast.78, f32[]{:T(128)} %constant.34.clone.1), kind=kCustom, calls=%fused_computation.46 | custom fusion | bytes 262148
  285.3 1.9 collective-permute-start.5
  287.2 0.9 convolution_bitcast_fusion
  288.4 25.6 %psum.15 = f32[16,48]{1,0:T(8,128)S(1)} all-reduce(f32[16,48]{1,0:T(8,128)S(1)} %convolution_bitcast_fusion.1), channel_id=1, replica_groups=mesh['frames'=8,'slabs'=64] {'frames'}, use_global_device_ids=true, to_apply=%region_1.0 | all-reduce | flops 768 | bytes 6144 | tf_op jit(solution)/shard_map/psum | solution.py:80
  314.1 0.7 gather_fusion
  314.8 91.7 %all-reduce.2.cloned.1.call-done = f32[16,4096]{1,0:T(8,128)} async-done(((f32[16,4096]{1,0:T(8,128)}), f32[16,4096]{1,0:T(8,128)}) %all-reduce.2.cloned.1.call-update) | async-done | bytes 262160 | tf_op jit(solution)/shard_map/psum | solution.py:80
  406.5 5.8 while.20
  406.5 0.7 dynamic_slice.61
  408.6 0.3 convolution_add_fusion.8
  409.0 0.3 copy-done
  409.4 0.7 dynamic_slice.61
  411.0 0.3 convolution_add_fusion.9
  411.5 0.3 convolution_add_fusion.8
  411.9 0.3 copy-done
  412.4 11.1 %collective-permute-start.6 = (f32[16,2048]{1,0:T(8,128)S(1)}, f32[16,2048]{1,0:T(8,128)S(1)}, u32[]{:S(2)}, u32[]{:S(2)}) collective-permute-start(f32[16,2048]{1,0:T(8,128)S(1)} %get-tuple-element.138), channel_id=1, source_target_pairs={{0,1},{1,2},{2,3},{3,4},{4,5},{5,6},{6,7},{7,8},{8,9},{9,10},{10,1... | collective-permute-start | bytes 393224 | tf_op jit(solution)/shard_map/ppermute | solution.py:26
  423.5 2.1 collective-permute-start.7
  425.7 3.9 collective-permute-done.6
  429.6 9.0 %collective-permute-done.7 = f32[16,2048]{1,0:T(8,128)S(1)} collective-permute-done((f32[16,2048]{1,0:T(8,128)S(1)}, f32[16,2048]{1,0:T(8,128)S(1)}, u32[]{:S(2)}, u32[]{:S(2)}) %collective-permute-start.7) | collective-permute-done | bytes 131104 | tf_op jit(solution)/shard_map/ppermute | solution.py:26
  438.6 5.0 while.21
  438.6 0.6 dynamic_slice.67
  441.1 0.6 dynamic_slice.67
  443.6 258.4 %gather_fusion.1 = f32[32768]{0:T(1024)S(1)} fusion(f32[16,4096]{1,0:T(8,128)S(1)} %get-tuple-element.100, s32[32768]{0:T(1024)S(1)} %bitcast.39), kind=kCustom, calls=%fused_computation.1 | custom fusion | bytes 524288 | tf_op jit(solution)/shard_map/gather | solution.py:87
  702.0 0.7 reshape.25
  (67 shorter events, 4.7 us)
Async XLA Ops:
  6.5 19.9 %copy-start.6 = (s32[2]{0:T(128)S(1)}, s32[2]{0:T(128)}, u32[]{:S(2)}) copy-start(s32[2]{0:T(128)} %constant.49) | copy-start | bytes 28
  6.5 399.9 %all-reduce.2.cloned.1.call-start = ((), (), s32[]{:S(2)}) async-start(), calls=%async_computation | async-start | bytes 524288 | tf_op jit(solution)/shard_map/psum | solution.py:80
  6.5 281.6 %collective-permute-start.2 = (bf16[8,16]{1,0:T(8,128)(2,1)}, bf16[8,16]{1,0:T(8,128)(2,1)S(1)}, u32[]{:S(2)}, u32[]{:S(2)}) collective-permute-start(bf16[8,16]{1,0:T(8,128)(2,1)} %param.10), channel_id=1, source_target_pairs={{0,1},{1,2},{2,3},{3,4},{4,5},{5,6},{6,7},{7,8},{8,9},{9,10},{10,1... | collective-permute-start | bytes 776 | tf_op jit(solution)/shard_map/ppermute | solution.py:15
  23.5 264.7 %collective-permute-start.3 = (bf16[8,16]{1,0:T(8,128)(2,1)}, bf16[8,16]{1,0:T(8,128)(2,1)S(1)}, u32[]{:S(2)}, u32[]{:S(2)}) collective-permute-start(bf16[8,16]{1,0:T(8,128)(2,1)} %param.10), channel_id=1, source_target_pairs={{1,0},{2,1},{3,2},{4,3},{5,4},{6,5},{7,6},{8,7},{9,8},{10,9},{11,1... | collective-permute-start | bytes 776 | tf_op jit(solution)/shard_map/ppermute | solution.py:18
  26.4 0.7 copy-start.7
  27.1 0.9 copy-start.4
  148.3 12.4 %copy-start.3 = (bf16[8,2048]{1,0:T(8,128)(2,1)S(1)}, bf16[8,2048]{1,0:T(8,128)(2,1)}, u32[]{:S(2)}) copy-start(bf16[8,2048]{1,0:T(8,128)(2,1)} %param.9) | copy-start | bytes 98308
  148.3 166.5 %collective-permute-start.4 = (f32[16,2048]{1,0:T(8,128)S(1)}, f32[16,2048]{1,0:T(8,128)S(1)}, u32[]{:S(2)}, u32[]{:S(2)}) collective-permute-start(f32[16,2048]{1,0:T(8,128)S(1)} %get-tuple-element.140), channel_id=1, source_target_pairs={{0,1},{1,2},{2,3},{3,4},{4,5},{5,6},{6,7},{7,8},{8,9},{9,10},{10,1... | collective-permute-start | bytes 393224 | tf_op jit(solution)/shard_map/ppermute | solution.py:26
  160.7 124.6 %collective-permute-start = (bf16[8,1024]{1,0:T(8,128)(2,1)S(1)}, bf16[8,1024]{1,0:T(8,128)(2,1)S(1)}, u32[]{:S(2)}, u32[]{:S(2)}) collective-permute-start(bf16[8,1024]{1,0:T(8,128)(2,1)S(1)} %get-tuple-element.141), channel_id=1, source_target_pairs={{0,1},{1,2},{2,3},{3,4},{4,5},{5,6},{6,7},{7,8},{8,9},{9,10},{10,1... | collective-permute-start | bytes 49160 | tf_op jit(solution)/shard_map/ppermute | solution.py:15
  162.6 124.6 %collective-permute-start.1 = (bf16[8,1024]{1,0:T(8,128)(2,1)S(1)}, bf16[8,1024]{1,0:T(8,128)(2,1)S(1)}, u32[]{:S(2)}, u32[]{:S(2)}) collective-permute-start(bf16[8,1024]{1,0:T(8,128)(2,1)S(1)} %get-tuple-element.142), channel_id=1, source_target_pairs={{1,0},{2,1},{3,2},{4,3},{5,4},{6,5},{7,6},{8,7},{9,8},{10,9},{11,1... | collective-permute-start | bytes 49160 | tf_op jit(solution)/shard_map/ppermute | solution.py:18
  285.2 2.0 copy-start.5
  285.3 29.5 %collective-permute-start.5 = (f32[16,2048]{1,0:T(8,128)S(1)}, f32[16,2048]{1,0:T(8,128)S(1)}, u32[]{:S(2)}, u32[]{:S(2)}) collective-permute-start(f32[16,2048]{1,0:T(8,128)S(1)} %get-tuple-element.139), channel_id=1, source_target_pairs={{1,0},{2,1},{3,2},{4,3},{5,4},{6,5},{7,6},{8,7},{9,8},{10,9},{11,1... | collective-permute-start | bytes 393224 | tf_op jit(solution)/shard_map/ppermute | solution.py:26
  314.1 92.4 %copy-start.8 = (s32[2]{0:T(128)S(1)}, s32[2]{0:T(128)}, u32[]{:S(2)}) copy-start(s32[2]{0:T(128)} %param.13) | copy-start | bytes 28
  408.3 1.0 copy-start
  411.3 1.0 copy-start
  412.3 13.2 %copy-start.2 = (s32[16,2048]{1,0:T(8,128)S(1)}, s32[16,2048]{1,0:T(8,128)}, u32[]{:S(2)}) copy-start(s32[16,2048]{1,0:T(8,128)} %param.11) | copy-start | bytes 393220
  412.4 17.2 %collective-permute-start.6 = (f32[16,2048]{1,0:T(8,128)S(1)}, f32[16,2048]{1,0:T(8,128)S(1)}, u32[]{:S(2)}, u32[]{:S(2)}) collective-permute-start(f32[16,2048]{1,0:T(8,128)S(1)} %get-tuple-element.138), channel_id=1, source_target_pairs={{0,1},{1,2},{2,3},{3,4},{4,5},{5,6},{6,7},{7,8},{8,9},{9,10},{10,1... | collective-permute-start | bytes 393224 | tf_op jit(solution)/shard_map/ppermute | solution.py:26
  423.5 15.1 %copy-start.1 = (f32[16,4096]{1,0:T(8,128)S(1)}, f32[16,4096]{1,0:T(8,128)}, u32[]{:S(2)}) copy-start(f32[16,4096]{1,0:T(8,128)} %get-tuple-element.334) | copy-start | bytes 786436
  423.5 15.1 %collective-permute-start.7 = (f32[16,2048]{1,0:T(8,128)S(1)}, f32[16,2048]{1,0:T(8,128)S(1)}, u32[]{:S(2)}, u32[]{:S(2)}) collective-permute-start(f32[16,2048]{1,0:T(8,128)S(1)} %get-tuple-element.137), channel_id=1, source_target_pairs={{1,0},{2,1},{3,2},{4,3},{5,4},{6,5},{7,6},{8,7},{9,8},{10,9},{11,1... | collective-permute-start | bytes 393224 | tf_op jit(solution)/shard_map/ppermute | solution.py:26
Sparse Core Ops, SparseCore 0:
  288.3 118.1 all-reduce.1
where the time goes:
time: 712 us; the launch traced here: 710 us
  local copies, waits for them, and re-layouts  505 us (71%)
  waiting for transfers between devices  105 us (15%)
  starting transfers between devices  50.6 us (7%)
  blocking collectives  25.6 us (4%)
  between operations  13.7 us (2%)
    gather x2, local copies, waits for them, and re-layouts, local(): return dense[rows, voxel_index]  259 us
    unnamed x22, local copies, waits for them, and re-layouts  242 us
    psum x1, waiting for transfers between devices, local(): stat, gram = lax.psum((stat_part, gram_part), 'frames')  91.7 us
    ppermute x4, starting transfers between devices, shifted(): lax.ppermute(value, axis, [(source, source + steps) for source in range(l...  27.4 us
    psum x1, blocking collectives, local(): stat, gram = lax.psum((stat_part, gram_part), 'frames')  25.6 us
    ppermute x2, starting transfers between devices, padded(): lax.ppermute(lax.slice_in_dim(block, block.shape[dim] - width, None, axis...  18.9 us
  transfers between devices with their start and end apart: 9, of which 3 were waited for; matrix products, arithmetic and copies ran while one was open for 34% of the time, Pallas kernels for 0%

commit v1 on v0

v1 whole, which is shorter than its diff:
```python
import functools

import jax
import jax.numpy as jnp
from jax import lax
from jax.experimental import pallas as pl
from jax.experimental.pallas import tpu as pltpu
from jax.sharding import PartitionSpec as P

F32 = jnp.float32
BF16 = jnp.bfloat16
BLOCK = 8
LANES = 128
FAR = 4


def scatter_kernel(idx_ref, val_ref, out_ref, rows_ref):
    sources, count = idx_ref.shape
    tiles = out_ref.shape[1] // LANES
    tile_ids = lax.broadcasted_iota(jnp.int32, (tiles, count), 0)
    lane_ids = lax.broadcasted_iota(jnp.int32, (LANES, count), 0)
    for k in range(sources):
        pos = idx_ref[k : k + 1, :]
        val = val_ref[k : k + 1, :]
        top = val.astype(BF16).astype(F32)
        rest = val - top
        mid = rest.astype(BF16).astype(F32)
        low = rest - mid
        in_tile = tile_ids == (pos >> 7)
        on_lane = (lane_ids == (pos & (LANES - 1))).astype(F32).astype(BF16)
        left = jnp.concatenate(
            [
                jnp.where(in_tile, part, 0.0)
                for part in (top, mid, low, jnp.ones_like(val))
            ],
            axis=0,
        ).astype(BF16)
        found = lax.dot_general(
            left, on_lane, (((1,), (1,)), ((), ())), preferred_element_type=F32
        )
        value = found[:tiles] + (found[tiles : 2 * tiles] + found[2 * tiles : 3 * tiles])
        rows_ref[k * tiles : (k + 1) * tiles, :] = jnp.where(
            found[3 * tiles :] > 0.5, value, -1.0
        )
    for t in range(tiles):
        out_ref[:, t * LANES : (t + 1) * LANES] = rows_ref[pl.ds(t, sources, stride=tiles), :]


def scatter(voxel_index, footprint, extent):
    sources, _ = voxel_index.shape
    return pl.pallas_call(
        scatter_kernel,
        out_shape=jax.ShapeDtypeStruct((sources, extent), F32),
        scratch_shapes=[pltpu.VMEM((sources * extent // LANES, LANES), F32)],
        cost_estimate=pl.CostEstimate(flops=8_000_000_000, bytes_accessed=524288, transcendentals=0),
    )(voxel_index, footprint)


def parts_of(x):
    top = x.astype(BF16).astype(F32)
    return top, x - top


def weights(g):
    top, low = parts_of(g)
    packed = top + pltpu.roll(low, 32, 1) + pltpu.roll(top, 64, 1) + pltpu.roll(low, 96, 1)
    return packed.astype(BF16)


def pull(packed, x):
    top, low = parts_of(x)
    top, low = top.astype(BF16), low.astype(BF16)
    stacked = jnp.concatenate([top, top, low, low], axis=0)
    return jnp.dot(packed, stacked, preferred_element_type=F32)


def sweep_kernel(far_ref, order_ref, data_ref, own_ref, low_ref, high_ref, idx_ref, out_ref,
                 movie_ref, turned_ref, dense_ref):
    groups, pairs, rows, _ = data_ref.shape
    frames = groups * pairs * rows
    sources, extent = own_ref.shape
    half = extent // 2
    margin = half // 2
    far_low, far_high = far_ref[0], far_ref[1]

    lane = lax.broadcasted_iota(jnp.int32, (rows, LANES), 1)
    pieces = []
    for g in range(groups):
        for b in range(pairs):
            at = (g * pairs + b) * rows
            lo = b ^ far_low
            hi = b ^ far_high
            movie_ref[at : at + rows, :margin] = data_ref[g, lo, :, :margin].astype(F32)
            movie_ref[at : at + rows, margin : 3 * margin] = data_ref[g, b, :, margin : 3 * margin].astype(F32)
            movie_ref[at : at + rows, 3 * margin :] = data_ref[g, hi, :, 3 * margin : extent].astype(F32)
            pieces.append(
                jnp.where(
                    lane < sources,
                    data_ref[g, lo, :, extent:].astype(F32),
                    jnp.where(
                        lane < 2 * sources,
                        data_ref[g, b, :, extent:].astype(F32),
                        data_ref[g, hi, :, extent:].astype(F32),
                    ),
                )
            )
    turned_ref[...] = jnp.transpose(jnp.concatenate(pieces, axis=0))
    first = pl.multiple_of(order_ref[0] * BLOCK, BLOCK)
    second = pl.multiple_of(order_ref[1] * BLOCK, BLOCK)
    turned = jnp.concatenate(
        [turned_ref[pl.ds(base + at, BLOCK), :] for base in (0, sources, 2 * sources) for at in (first, second)]
        + [jnp.zeros((LANES - 3 * sources, frames), F32)],
        axis=0,
    ).astype(BF16)
    gram = lax.dot_general(turned, turned, (((1,), (1,)), ((), ())), preferred_element_type=F32)
    here = lax.broadcasted_iota(jnp.int32, (LANES, LANES), 0)
    there = lax.broadcasted_iota(jnp.int32, (LANES, LANES), 1)
    scale = jnp.sum(jnp.where(here == there, gram, 0.0), axis=1, keepdims=True) + 1.0
    inverse = 1.0 / scale

    def fresh(old, held, stat, pulled, inv):
        return jnp.where(held, jnp.maximum(old + (stat - pulled) * inv, 0.0), 0.0)

    live = lax.broadcasted_iota(jnp.int32, (2 * sources, LANES), 1) < 2 * sources
    for side in range(2):
        base = side * sources
        cols = pl.ds(side * half, half)
        g = gram[base : base + 2 * sources]
        if side:
            g = pltpu.roll(g, LANES - base, 1)
        g = jnp.where(live, g, 0.0)
        inv = inverse[base : base + 2 * sources]
        stat = jnp.dot(
            turned[base : base + 2 * sources],
            movie_ref[:, cols].astype(BF16),
            preferred_element_type=F32,
        )
        near_ref = high_ref if side else low_ref
        mine = [own_ref[pl.ds(at, BLOCK), cols] for at in (first, second)]
        near = [near_ref[pl.ds(at, BLOCK), :] for at in (first, second)]
        raw = mine + near if side else near + mine
        held = [r >= 0.0 for r in raw]
        x = [jnp.maximum(r, 0.0) for r in raw]
        s = [stat[i * BLOCK : (i + 1) * BLOCK] for i in range(4)]
        v = [inv[i * BLOCK : (i + 1) * BLOCK] for i in range(4)]
        packed = weights(g)
        inside = jnp.where(
            (lax.broadcasted_iota(jnp.int32, g.shape, 0) // sources)
            == (lax.broadcasted_iota(jnp.int32, g.shape, 1) // sources),
            g,
            0.0,
        )
        inside = weights(inside)
        zero = jnp.zeros_like(x[0])
        p = pull(packed, jnp.concatenate(x, axis=0))
        p = [p[i * BLOCK : (i + 1) * BLOCK] for i in range(4)]
        new = list(x)
        for i in (0, 2):
            new[i] = fresh(x[i], held[i], s[i], p[i], v[i])
        more = pull(inside, jnp.concatenate([new[0] - x[0], zero, new[2] - x[2], zero], axis=0))
        for i in (1, 3):
            new[i] = fresh(x[i], held[i], s[i], p[i] + more[i * BLOCK : (i + 1) * BLOCK], v[i])
        a = 0 if side else 2
        p = pull(packed, jnp.concatenate(new, axis=0))
        last = fresh(new[a], held[a], s[a], p[a * BLOCK : (a + 1) * BLOCK], v[a])
        change = [zero] * 4
        change[a] = last - new[a]
        more = pull(inside, jnp.concatenate(change, axis=0))
        b = a + 1
        rows_b = slice(b * BLOCK, (b + 1) * BLOCK)
        final = fresh(new[b], held[b], s[b], p[rows_b] + more[rows_b], v[b])
        dense_ref[pl.ds(first, BLOCK), cols] = last
        dense_ref[pl.ds(second, BLOCK), cols] = final

    for r in range(0, sources, BLOCK):
        table = [dense_ref[r : r + BLOCK, t * LANES : (t + 1) * LANES] for t in range(extent // LANES)]
        for c in range(0, idx_ref.shape[1], LANES):
            pos = idx_ref[r : r + BLOCK, c : c + LANES]
            tile = pos >> 7
            at = pos & (LANES - 1)
            got = jnp.zeros((BLOCK, LANES), F32)
            for t in range(extent // LANES):
                got = jnp.where(tile == t, jnp.take_along_axis(table[t], at, axis=1), got)
            out_ref[r : r + BLOCK, c : c + LANES] = got


def sweeps(far, order, data, own, low, high, voxel_index):
    sources, extent = own.shape
    groups, pairs, rows, _ = data.shape
    smem = pl.BlockSpec(memory_space=pltpu.SMEM)
    vmem = pl.BlockSpec(memory_space=pltpu.VMEM)
    return pl.pallas_call(
        sweep_kernel,
        out_shape=jax.ShapeDtypeStruct(voxel_index.shape, F32),
        in_specs=[smem, smem] + [vmem] * 5,
        out_specs=vmem,
        scratch_shapes=[
            pltpu.VMEM((groups * pairs * rows, extent), F32),
            pltpu.VMEM((LANES, groups * pairs * rows), F32),
            pltpu.VMEM((sources, extent), F32),
        ],
    )(far, order, data, own, low, high, voxel_index)


def joint(frames, slabs, step):
    pairs = []
    for f in range(frames):
        for s in range(slabs):
            if 0 <= s + step < slabs:
                odd = s % 2 if step > 0 else (s + 1) % 2
                pairs.append((f * slabs + s, (f ^ (FAR * odd)) * slabs + s + step))
    return pairs


def local(sizes, movie, traces, voxel_index, footprint, block_order):
    frames, slabs = sizes
    both = ("frames", "slabs")
    up, down = joint(frames, slabs, 1), joint(frames, slabs, -1)
    voxels = movie.shape[1]
    half = voxels // 2
    sources = traces.shape[1]
    extent = 2 * voxels
    padded = jnp.pad(traces, ((0, 0), (0, LANES - sources)))
    low = lax.ppermute(jnp.concatenate([movie[:, half:], padded], axis=1), both, up)
    high = lax.ppermute(jnp.concatenate([movie[:, :half], padded], axis=1), both, down)
    dense = scatter(voxel_index, footprint, extent)
    low_dense = lax.ppermute(dense[:, voxels:], both, up)
    high_dense = lax.ppermute(dense[:, :voxels], both, down)
    mine = jnp.concatenate(
        [
            low[:, :half], movie, high[:, :half],
            low[:, half : half + sources], traces, high[:, half : half + sources],
            jnp.zeros((movie.shape[0], LANES - 3 * sources), movie.dtype),
        ],
        axis=1,
    )
    other = lax.ppermute(mine, "frames", [(f, f ^ FAR) for f in range(frames)])
    pair = jnp.stack([mine, other])
    data = lax.all_to_all(
        jnp.broadcast_to(pair[None], (FAR,) + pair.shape), "frames", 0, 0,
        axis_index_groups=[list(range(a, a + FAR)) for a in range(0, frames, FAR)],
    )
    odd = lax.rem(lax.axis_index("slabs"), 2)
    far = jnp.stack([1 - odd, odd]).astype(jnp.int32)
    return sweeps(far, block_order, data, dense, low_dense, high_dense, voxel_index)


def solution(mesh):
    sizes = (mesh.shape["frames"], mesh.shape["slabs"])
    in_specs = (P("frames", "slabs"), P("frames", "slabs"), P("slabs", None), P("slabs", None), P())
    return jax.shard_map(
        functools.partial(local, sizes), mesh=mesh, in_specs=in_specs,
        out_specs=P("slabs", None), check_vma=False,
    )
```

time: 712 us -> 70.9 us (0.10)
  the two profiles are of different devices: /device:TPU:1 before, /device:TPU:88 now
where the time goes in v1:
time: 70.9 us; the launch traced here: 70.3 us
  starting transfers between devices  41.1 us (58%)
  waiting for transfers between devices  13 us (18%)
  Pallas kernels  9.23 us (13%)
  local copies, waits for them, and re-layouts  6.12 us (9%)
    ppermute x1, starting transfers between devices, local(): lax.ppermute(jnp.concatenate([movie[:, :half], padded], axis=1), both, down)  12.8 us
    ppermute x1, starting transfers between devices, local(): high_dense = lax.ppermute(dense[:, :voxels], both, down)  9.04 us
    ppermute x1, waiting for transfers between devices, local(): low_dense = lax.ppermute(dense[:, voxels:], both, up)  8.12 us
    all_to_all x1, starting transfers between devices, local(): lax.all_to_all(jnp.broadcast_to(pair[None], (FAR,) + pair.shape), 'frames...  7.1 us
    ppermute x1, starting transfers between devices, local(): other = lax.ppermute(mine, 'frames', [(f, f ^ FAR) for f in range(frames)])  6.89 us
    pallas_call x1, Pallas kernels, sweeps(): pl.pallas_call(sweep_kernel, out_shape=jax.ShapeDtypeStruct(voxel_index.s...  4.8 us
    pallas_call x1, Pallas kernels, scatter(): pl.pallas_call(scatter_kernel, out_shape=jax.ShapeDtypeStruct((sources, e...  4.43 us
    ppermute x1, waiting for transfers between devices, local(): other = lax.ppermute(mine, 'frames', [(f, f ^ FAR) for f in range(frames)])  4.1 us
  transfers between devices with their start and end apart: 6, of which 3 were waited for; matrix products, arithmetic and copies ran while one was open for 2% of the time, Pallas kernels for 6%

profile of v1, /device:TPU:88, one launch (start us, length us, event | category | flops | bytes accessed | tf_op | source)
XLA Modules:
  0.0 70.3 jit_solution(5234108618454629630)
XLA Ops:
  0.0 0.7 %fusion.4 = (bf16[8,1024]{1,0:T(8,128)(2,1)S(1)}, bf16[8,1024]{1,0:T(8,128)(2,1)S(1)}) fusion(bf16[8,2048]{1,0:T(8,128)(2,1)} %param.5), kind=kLoop, calls=%fused_computation.7 | loop fusion | bytes 65536 | tf_op jit(solution)/shard_map/slice | solution.py:225
  0.7 0.0 copy-start.5
  0.7 0.7 copy-done.5
  1.4 1.9 %collective-permute-start = (bf16[8,1152]{1,0:T(8,128)(2,1)S(1)}, bf16[8,1152]{1,0:T(8,128)(2,1)S(1)}, u32[]{:S(2)}, u32[]{:S(2)}) collective-permute-start(bf16[8,1152]{1,0:T(8,128)(2,1)S(1)} %get-tuple-element.10), channel_id=1, source_target_pairs={{0,1},{1,258},{2,3},{3,260},{4,5},{5,262},{6,7},{7,264},{8,9},{9,2... | collective-permute-start | bytes 55304 | tf_op jit(solution)/shard_map/ppermute | solution.py:224
  3.3 0.0 copy-start.3
  3.4 12.8 %collective-permute-start.1 = (bf16[8,1152]{1,0:T(8,128)(2,1)S(1)}, bf16[8,1152]{1,0:T(8,128)(2,1)S(1)}, u32[]{:S(2)}, u32[]{:S(2)}) collective-permute-start(bf16[8,1152]{1,0:T(8,128)(2,1)S(1)} %get-tuple-element.9), channel_id=1, source_target_pairs={{1,0},{2,257},{3,2},{4,259},{5,4},{6,261},{7,6},{8,263},{9,8},{10,... | collective-permute-start | bytes 55304 | tf_op jit(solution)/shard_map/ppermute | solution.py:225
  16.1 0.0 collective-permute-done
  16.1 0.0 copy-start.4
  16.1 0.6 copy-done.4
  16.7 0.8 %collective-permute-done.1 = bf16[8,1152]{1,0:T(8,128)(2,1)S(1)} collective-permute-done((bf16[8,1152]{1,0:T(8,128)(2,1)S(1)}, bf16[8,1152]{1,0:T(8,128)(2,1)S(1)}, u32[]{:S(2)}, u32[]{:S(2)}) %collective-permute-start.1) | collective-permute-done | bytes 18464 | tf_op jit(solution)/shard_map/ppermute | solution.py:225
  17.6 0.0 slice-start
  17.6 0.0 slice-start.1
  17.6 0.0 copy-done.3
  17.6 0.7 slice-done
  18.3 0.0 slice-done.1
  18.3 0.1 concatenate.11
  18.4 6.9 %collective-permute-start.2 = (bf16[8,4224]{1,0:T(8,128)(2,1)S(1)}, bf16[8,4224]{1,0:T(8,128)(2,1)S(1)}, u32[]{:S(2)}, u32[]{:S(2)}) collective-permute-start(bf16[8,4224]{1,0:T(8,128)(2,1)S(1)} %concatenate.11), channel_id=1, source_target_pairs={{0,256},{64,320},{128,384},{192,448},{256,0},{320,64},{384,128},{4... | collective-permute-start | bytes 202760 | tf_op jit(solution)/shard_map/ppermute | solution.py:237
  25.3 4.1 %collective-permute-done.2 = bf16[8,4224]{1,0:T(8,128)(2,1)S(1)} collective-permute-done((bf16[8,4224]{1,0:T(8,128)(2,1)S(1)}, bf16[8,4224]{1,0:T(8,128)(2,1)S(1)}, u32[]{:S(2)}, u32[]{:S(2)}) %collective-permute-start.2) | collective-permute-done | bytes 67616 | tf_op jit(solution)/shard_map/ppermute | solution.py:237
  29.4 0.8 %broadcast_in_dim.10 = bf16[4,2,8,4224]{3,2,1,0:T(8,128)(2,1)} broadcast(bf16[2,8,4224]{2,1,0:T(8,128)(2,1)S(1)} %pad_maximum_fusion), dimensions={1,2,3} | broadcast | bytes 675840 | tf_op jit(solution)/shard_map/broadcast_in_dim | solution.py:240
  30.2 7.1 %all-to-all-start = ((bf16[4,2,8,4224]{3,2,1,0:T(8,128)(2,1)}), bf16[4,2,8,4224]{3,2,1,0:T(8,128)(2,1)S(1)}, u32[]{:S(2)}, u32[]{:S(2)}) async-start(bf16[4,2,8,4224]{3,2,1,0:T(8,128)(2,1)} %broadcast_in_dim.10), calls=%async_computation | async-start | bytes 1081344 | tf_op jit(solution)/shard_map/all_to_all | solution.py:239
  37.3 4.4 %shard_map.55.own_ref = f32[16,4096]{1,0:T(8,128)} custom-call(s32[16,2048]{1,0:T(8,128)} %idx_ref.3, f32[16,2048]{1,0:T(8,128)} %val_ref.1), custom_call_target="tpu_custom_call" | custom-call | flops 8000000000 | bytes 524288 | tf_op jit(solution)/shard_map/pallas_call | solution.py:51
  41.8 1.0 %fusion.3 = (f32[16,2048]{1,0:T(8,128)S(1)}, f32[16,2048]{1,0:T(8,128)S(1)}) fusion(f32[16,4096]{1,0:T(8,128)} %shard_map.55.own_ref), kind=kLoop, calls=%fused_computation.6 | loop fusion | bytes 524288 | tf_op jit(solution)/shard_map/slice | solution.py:228
  42.8 3.4 %collective-permute-start.3 = (f32[16,2048]{1,0:T(8,128)S(1)}, f32[16,2048]{1,0:T(8,128)S(1)}, u32[]{:S(2)}, u32[]{:S(2)}) collective-permute-start(f32[16,2048]{1,0:T(8,128)S(1)} %get-tuple-element.6), channel_id=1, source_target_pairs={{0,1},{1,258},{2,3},{3,260},{4,5},{5,262},{6,7},{7,264},{8,9},{9,2... | collective-permute-start | bytes 393224 | tf_op jit(solution)/shard_map/ppermute | solution.py:227
  46.2 9.0 %collective-permute-start.4 = (f32[16,2048]{1,0:T(8,128)S(1)}, f32[16,2048]{1,0:T(8,128)S(1)}, u32[]{:S(2)}, u32[]{:S(2)}) collective-permute-start(f32[16,2048]{1,0:T(8,128)S(1)} %get-tuple-element.5), channel_id=1, source_target_pairs={{1,0},{2,257},{3,2},{4,259},{5,4},{6,261},{7,6},{8,263},{9,8},{10,... | collective-permute-start | bytes 393224 | tf_op jit(solution)/shard_map/ppermute | solution.py:228
  55.3 0.7 pad_add_fusion.far_ref
  55.9 8.1 %collective-permute-done.3.low_ref = f32[16,2048]{1,0:T(8,128)S(1)} collective-permute-done((f32[16,2048]{1,0:T(8,128)S(1)}, f32[16,2048]{1,0:T(8,128)S(1)}, u32[]{:S(2)}, u32[]{:S(2)}) %collective-permute-start.3) | collective-permute-done | bytes 131104 | tf_op jit(solution)/shard_map/ppermute | solution.py:227
  64.0 0.0 collective-permute-done.4.high_ref
  64.0 0.0 all-to-all-done.data_ref
  64.0 0.6 copy-done.1
  64.7 0.0 copy-done.2
  64.7 0.8 %copy-done = bf16[4,2,8,4224]{3,2,1,0:T(8,128)(2,1)} copy-done((bf16[4,2,8,4224]{3,2,1,0:T(8,128)(2,1)}, bf16[4,2,8,4224]{3,2,1,0:T(8,128)(2,1)S(1)}, u32[]{:S(2)}) %copy-start) | copy-done | bytes 540696
  65.5 4.8 %shard_map.56 = f32[16,2048]{1,0:T(8,128)} custom-call(s32[2]{0:T(128)} %pad_add_fusion.far_ref, s32[2]{0:T(128)} %order_ref.1, bf16[4,2,8,4224]{3,2,1,0:T(8,128)(2,1)} %copy-done, f32[16,4096]{1,0:T(8,128)} %shard_map.55.own_ref, f32[16,2048]{1,0:T(8,128)} %copy-done.1, f32[16,2048]{1,0:T(8,128)} %copy-done.2, s32[16,2048]{1,0:T(8,128)} %idx_ref.3), custom_call_target="tpu_custom_call" | custom-call | tf_op jit(solution)/shard_map/pallas_call | solution.py:192
  (8 shorter events, 0.0 us)
Async XLA Ops:
  0.7 0.7 copy-start.5
  1.4 14.7 %collective-permute-start = (bf16[8,1152]{1,0:T(8,128)(2,1)S(1)}, bf16[8,1152]{1,0:T(8,128)(2,1)S(1)}, u32[]{:S(2)}, u32[]{:S(2)}) collective-permute-start(bf16[8,1152]{1,0:T(8,128)(2,1)S(1)} %get-tuple-element.10), channel_id=1, source_target_pairs={{0,1},{1,258},{2,3},{3,260},{4,5},{5,262},{6,7},{7,264},{8,9},{9,2... | collective-permute-start | bytes 55304 | tf_op jit(solution)/shard_map/ppermute | solution.py:224
  3.3 14.2 %copy-start.3 = (bf16[8,2048]{1,0:T(8,128)(2,1)S(1)}, bf16[8,2048]{1,0:T(8,128)(2,1)}, u32[]{:S(2)}) copy-start(bf16[8,2048]{1,0:T(8,128)(2,1)} %param.5) | copy-start | bytes 98308
  3.4 14.2 %collective-permute-start.1 = (bf16[8,1152]{1,0:T(8,128)(2,1)S(1)}, bf16[8,1152]{1,0:T(8,128)(2,1)S(1)}, u32[]{:S(2)}, u32[]{:S(2)}) collective-permute-start(bf16[8,1152]{1,0:T(8,128)(2,1)S(1)} %get-tuple-element.9), channel_id=1, source_target_pairs={{1,0},{2,257},{3,2},{4,259},{5,4},{6,261},{7,6},{8,263},{9,8},{10,... | collective-permute-start | bytes 55304 | tf_op jit(solution)/shard_map/ppermute | solution.py:225
  16.1 0.6 copy-start.4
  17.6 0.7 %slice-start = ((bf16[8,1152]{1,0:T(8,128)(2,1)}), bf16[8,1024]{1,0:T(8,128)(2,1)S(1)}, s32[]{:S(2)}) async-start(bf16[8,1152]{1,0:T(8,128)(2,1)} %copy-done.4), calls=%async_computation.1 | async-start | bytes 32768 | tf_op jit(solution)/shard_map/slice | solution.py:231
  17.6 0.7 %slice-start.1 = ((bf16[8,1152]{1,0:T(8,128)(2,1)}), bf16[8,16]{1,0:T(8,128)(2,1)S(1)}, s32[]{:S(2)}) async-start(bf16[8,1152]{1,0:T(8,128)(2,1)} %copy-done.4), calls=%async_computation.2 | async-start | bytes 4096 | tf_op jit(solution)/shard_map/slice | solution.py:232
  18.4 11.0 %collective-permute-start.2 = (bf16[8,4224]{1,0:T(8,128)(2,1)S(1)}, bf16[8,4224]{1,0:T(8,128)(2,1)S(1)}, u32[]{:S(2)}, u32[]{:S(2)}) collective-permute-start(bf16[8,4224]{1,0:T(8,128)(2,1)S(1)} %concatenate.11), channel_id=1, source_target_pairs={{0,256},{64,320},{128,384},{192,448},{256,0},{320,64},{384,128},{4... | collective-permute-start | bytes 202760 | tf_op jit(solution)/shard_map/ppermute | solution.py:237
  30.2 33.8 %all-to-all-start = ((bf16[4,2,8,4224]{3,2,1,0:T(8,128)(2,1)}), bf16[4,2,8,4224]{3,2,1,0:T(8,128)(2,1)S(1)}, u32[]{:S(2)}, u32[]{:S(2)}) async-start(bf16[4,2,8,4224]{3,2,1,0:T(8,128)(2,1)} %broadcast_in_dim.10), calls=%async_computation | async-start | bytes 1081344 | tf_op jit(solution)/shard_map/all_to_all | solution.py:239
  42.8 21.3 %collective-permute-start.3 = (f32[16,2048]{1,0:T(8,128)S(1)}, f32[16,2048]{1,0:T(8,128)S(1)}, u32[]{:S(2)}, u32[]{:S(2)}) collective-permute-start(f32[16,2048]{1,0:T(8,128)S(1)} %get-tuple-element.6), channel_id=1, source_target_pairs={{0,1},{1,258},{2,3},{3,260},{4,5},{5,262},{6,7},{7,264},{8,9},{9,2... | collective-permute-start | bytes 393224 | tf_op jit(solution)/shard_map/ppermute | solution.py:227
  46.2 17.8 %collective-permute-start.4 = (f32[16,2048]{1,0:T(8,128)S(1)}, f32[16,2048]{1,0:T(8,128)S(1)}, u32[]{:S(2)}, u32[]{:S(2)}) collective-permute-start(f32[16,2048]{1,0:T(8,128)S(1)} %get-tuple-element.5), channel_id=1, source_target_pairs={{1,0},{2,257},{3,2},{4,259},{5,4},{6,261},{7,6},{8,263},{9,8},{10,... | collective-permute-start | bytes 393224 | tf_op jit(solution)/shard_map/ppermute | solution.py:228
  64.0 0.6 copy-start.1
  64.0 0.7 copy-start.2
  64.7 0.8 %copy-start = (bf16[4,2,8,4224]{3,2,1,0:T(8,128)(2,1)}, bf16[4,2,8,4224]{3,2,1,0:T(8,128)(2,1)S(1)}, u32[]{:S(2)}) copy-start(bf16[4,2,8,4224]{3,2,1,0:T(8,128)(2,1)S(1)} %all-to-all-done.data_ref) | copy-start | bytes 1622020

commit v2 on v0

v2 whole, which is shorter than its diff:
```python
import functools

import jax
import jax.numpy as jnp
from jax import lax
from jax.experimental import pallas as pl
from jax.experimental.pallas import tpu as pltpu
from jax.sharding import PartitionSpec as P

F32 = jnp.float32
BF16 = jnp.bfloat16
BLOCK = 8
LANES = 128
FAR = 4


def call(body, out_shape, scalars, arrays, scratch=(), limit=16):
    vmem = pl.BlockSpec(memory_space=pltpu.VMEM)
    smem = pl.BlockSpec(memory_space=pltpu.SMEM)
    return pl.pallas_call(
        body,
        out_shape=out_shape,
        in_specs=[smem] * len(scalars) + [vmem] * len(arrays),
        out_specs=jax.tree.map(lambda _: vmem, out_shape),
        scratch_shapes=list(scratch),
        compiler_params=pltpu.CompilerParams(vmem_limit_bytes=limit << 20),
    )(*scalars, *arrays)


def thirds(x):
    top = x.astype(BF16).astype(F32)
    rest = x - top
    mid = rest.astype(BF16).astype(F32)
    return top, mid, rest - mid


def front_kernel(where_ref, idx_ref, val_ref, movie_ref, traces_ref, out_ref, far_ref, near_ref, rows_ref):
    sources, count = idx_ref.shape
    tiles = 2 * far_ref.shape[1] // LANES
    odd, frame = where_ref[0], where_ref[1]
    tile_ids = lax.broadcasted_iota(jnp.int32, (tiles, count), 0)
    lane_ids = lax.broadcasted_iota(jnp.int32, (LANES, count), 0)
    for k in range(sources):
        pos = idx_ref[k : k + 1, :]
        val = val_ref[k : k + 1, :]
        in_tile = tile_ids == (pos >> 7)
        on_lane = (lane_ids == (pos & (LANES - 1))).astype(F32).astype(BF16)
        left = jnp.concatenate(
            [jnp.where(in_tile, part, 0.0) for part in thirds(val) + (jnp.ones_like(val),)], axis=0
        ).astype(BF16)
        found = lax.dot_general(left, on_lane, (((1,), (1,)), ((), ())), preferred_element_type=F32)
        value = found[:tiles] + (found[tiles : 2 * tiles] + found[2 * tiles : 3 * tiles])
        rows_ref[k * tiles : (k + 1) * tiles, :] = jnp.where(found[3 * tiles :] > 0.5, value, -1.0)
    for t in range(tiles // 2):
        cols = slice(t * LANES, (t + 1) * LANES)
        left = rows_ref[pl.ds(t, sources, stride=tiles), :]
        right = rows_ref[pl.ds(t + tiles // 2, sources, stride=tiles), :]
        far_ref[:, cols] = jnp.where(odd == 1, right, left)
        near_ref[:, cols] = jnp.where(odd == 1, left, right)

    rows, voxels = movie_ref.shape
    half = voxels // 2
    share = far_ref.shape[1] // 8
    at = odd * half
    far_half = movie_ref[:, pl.ds(pl.multiple_of(at, half), half)]
    near_half = movie_ref[:, pl.ds(pl.multiple_of(half - at, half), half)]
    tail = jnp.concatenate(
        [traces_ref[...].astype(F32), jnp.zeros((rows, LANES - sources), F32)], axis=1
    ).astype(BF16)
    piece = far_ref[:, pl.ds(pl.multiple_of(frame * share, share), share)]
    parts = [p[r : r + rows].astype(BF16) for p in parts_of(piece) for r in range(0, sources, rows)]
    mine = 2 * (1 - odd)
    for h in range(2):
        for slot in (mine + h, 2 - mine + h):
            out_ref[slot, :, :half] = far_half
            out_ref[slot, :, half : half + LANES] = tail
        out_ref[mine + h, :, half + LANES : 2 * half + LANES] = near_half
        for i, part in enumerate(parts):
            out_ref[2 - mine + h, :, pl.ds(half + LANES + i * share, share)] = part


def middle_kernel(where_ref, in_ref, out_ref):
    rows = in_ref.shape[1]
    half = (out_ref.shape[3] - in_ref.shape[2]) // 2
    odd, live = where_ref[0], where_ref[2]
    mine = 2 * (1 - odd)
    lane = lax.broadcasted_iota(jnp.int32, (rows, LANES), 1)
    for h in range(2):
        own, far = mine + h, 2 - mine + h
        far_half = in_ref[far, :, :half].astype(F32)
        far_half = jnp.where(live == 1, far_half, 0.0).astype(BF16)
        far_tail = jnp.where(live == 1, in_ref[far, :, half : half + LANES].astype(F32), 0.0)
        tail = (far_tail + pltpu.roll(in_ref[own, :, half : half + LANES].astype(F32), 16, 1)).astype(BF16)
        own_far = in_ref[own, :, :half]
        own_near = in_ref[own, :, half + LANES : 2 * half + LANES]
        dense = in_ref[far, :, half + LANES :]
        for g in range(FAR):
            out_ref[g, h, :, :half] = far_half
            out_ref[g, h, :, half : 2 * half] = own_far
            out_ref[g, h, :, 2 * half : 3 * half] = own_near
            out_ref[g, h, :, 3 * half : 3 * half + LANES] = tail
            out_ref[g, h, :, 3 * half + LANES :] = dense


def near_kernel(data_ref, dense_ref, out_ref):
    groups, pairs, rows, width = out_ref.shape
    sources, side = dense_ref.shape
    half = side // 2
    share = width - half - LANES
    for g in range(groups):
        for h in range(pairs):
            out_ref[g, h, :, :half] = data_ref[g, h, :, 2 * half : 3 * half].astype(F32)
            tail = data_ref[g, h, :, 3 * half : 3 * half + LANES].astype(F32)
            out_ref[g, h, :, half : half + LANES] = pltpu.roll(tail, LANES - 16, 1)
            out_ref[g, h, :, half + LANES :] = dense_ref[h * rows : (h + 1) * rows, g * share : (g + 1) * share]


def parts_of(x):
    top = x.astype(BF16).astype(F32)
    return top, x - top


def weights(g):
    top, low = parts_of(g)
    packed = top + pltpu.roll(low, 32, 1) + pltpu.roll(top, 64, 1) + pltpu.roll(low, 96, 1)
    return packed.astype(BF16)


def pull(packed, x):
    top, low = parts_of(x)
    top, low = top.astype(BF16), low.astype(BF16)
    stacked = jnp.concatenate([top, top, low, low], axis=0)
    return jnp.dot(packed, stacked, preferred_element_type=F32)


def both_sweeps(order_ref, tails, movie_ref, turned_ref, own_ref, other_ref, final_ref):
    sources = own_ref.shape[0]
    frames = movie_ref.shape[0]
    turned_ref[...] = jnp.transpose(jnp.concatenate(tails, axis=0))
    first = pl.multiple_of(order_ref[0] * BLOCK, BLOCK)
    second = pl.multiple_of(order_ref[1] * BLOCK, BLOCK)
    turned = jnp.concatenate(
        [turned_ref[pl.ds(base + at, BLOCK), :] for base in (0, sources) for at in (first, second)]
        + [jnp.zeros((LANES - 2 * sources, frames), F32)],
        axis=0,
    ).astype(BF16)
    gram = lax.dot_general(turned, turned, (((1,), (1,)), ((), ())), preferred_element_type=F32)[: 2 * sources]
    here = lax.broadcasted_iota(jnp.int32, gram.shape, 0)
    there = lax.broadcasted_iota(jnp.int32, gram.shape, 1)
    inverse = 1.0 / (jnp.sum(jnp.where(here == there, gram, 0.0), axis=1, keepdims=True) + 1.0)
    packed = weights(gram)
    inside = weights(jnp.where(here // sources == there // sources, gram, 0.0))
    stat = jnp.dot(turned[: 2 * sources], movie_ref[...].astype(BF16), preferred_element_type=F32)

    def cut(a):
        return [a[i * BLOCK : (i + 1) * BLOCK] for i in range(a.shape[0] // BLOCK)]

    raw = [ref[pl.ds(at, BLOCK), :] for ref in (other_ref, own_ref) for at in (first, second)]
    held = [r >= 0.0 for r in raw]
    x = [jnp.maximum(r, 0.0) for r in raw]
    s, v = cut(stat), cut(inverse)
    zero = jnp.zeros_like(x[0])

    def fresh(i, old, pulled):
        return jnp.where(held[i], jnp.maximum(old + (s[i] - pulled) * v[i], 0.0), 0.0)

    p = cut(pull(packed, jnp.concatenate(x, axis=0)))
    new = list(x)
    for i in (0, 2):
        new[i] = fresh(i, x[i], p[i])
    more = cut(pull(inside, jnp.concatenate([new[0] - x[0], zero, new[2] - x[2], zero], axis=0)))
    for i in (1, 3):
        new[i] = fresh(i, x[i], p[i] + more[i])
    p = cut(pull(packed[2 * BLOCK :], jnp.concatenate(new, axis=0)))
    last = fresh(2, new[2], p[0])
    more = pull(inside[3 * BLOCK :], jnp.concatenate([zero, zero, last - new[2], zero], axis=0))
    final = fresh(3, new[3], p[1] + more)
    final_ref[pl.ds(first, BLOCK), :] = last
    final_ref[pl.ds(second, BLOCK), :] = final


def pick(final_ref, idx_ref, out_ref, flip, base, start_ref):
    sources, half = final_ref.shape
    for r in range(0, sources, BLOCK):
        table = [final_ref[r : r + BLOCK, t * LANES : (t + 1) * LANES] for t in range(half // LANES)]
        for c in range(0, idx_ref.shape[1], LANES):
            pos = idx_ref[r : r + BLOCK, c : c + LANES] ^ flip
            tile = (pos >> 7) - base
            at = pos & (LANES - 1)
            got = jnp.zeros((BLOCK, LANES), F32) if start_ref is None else start_ref[r : r + BLOCK, c : c + LANES]
            for t in range(half // LANES):
                got = jnp.where(tile == t, jnp.take_along_axis(table[t], at, axis=1), got)
            out_ref[r : r + BLOCK, c : c + LANES] = got


def far_kernel(where_ref, order_ref, data_ref, own_ref, idx_ref, out_ref,
               movie_ref, turned_ref, other_ref, final_ref):
    groups, pairs, rows, _ = data_ref.shape
    sources, side = own_ref.shape
    half = side // 2
    share = side // 8
    odd = where_ref[0]
    halo_cols = pl.ds(pl.multiple_of(odd * half, half), half)
    own_cols = pl.ds(pl.multiple_of(half - odd * half, half), half)
    tails = []
    for g in range(groups):
        for h in range(pairs):
            at = pl.ds((g * pairs + h) * rows, rows)
            movie_ref[at, halo_cols] = data_ref[g, h, :, :half].astype(F32)
            movie_ref[at, own_cols] = data_ref[g, h, :, half : 2 * half].astype(F32)
            tails.append(data_ref[g, h, :, 3 * half : 3 * half + LANES].astype(F32))
            frame = g + FAR * h
            for i in range(sources // rows):
                top, low = [
                    data_ref[g, h, :, pl.ds(3 * half + LANES + (n * (sources // rows) + i) * share, share)].astype(F32)
                    for n in range(2)
                ]
                other_ref[i * rows : (i + 1) * rows, frame * share : (frame + 1) * share] = top + low
    both_sweeps(order_ref, tails, movie_ref, turned_ref, own_ref, other_ref, final_ref)
    pick(final_ref, idx_ref, out_ref, odd * side, 0, None)


def near_side_kernel(where_ref, order_ref, data_ref, halo_ref, own_ref, idx_ref, start_ref, out_ref,
                     movie_ref, turned_ref, final_ref, other_ref):
    groups, pairs, rows, _ = data_ref.shape
    sources, side = own_ref.shape
    half = side // 2
    odd = where_ref[0]
    own_cols = pl.ds(pl.multiple_of(odd * half, half), half)
    halo_cols = pl.ds(pl.multiple_of(half - odd * half, half), half)
    lane = lax.broadcasted_iota(jnp.int32, (rows, LANES), 1)
    tails = []
    for g in range(groups):
        for h in range(pairs):
            at = pl.ds((g * pairs + h) * rows, rows)
            movie_ref[at, halo_cols] = halo_ref[g, h, :, :half]
            share = side // groups
            other_ref[h * rows : (h + 1) * rows, g * share : (g + 1) * share] = halo_ref[g, h, :, half + LANES :]
            movie_ref[at, own_cols] = data_ref[g, h, :, 2 * half : 3 * half].astype(F32)
            tails.append(
                jnp.where(
                    lane < sources,
                    halo_ref[g, h, :, half : half + LANES],
                    data_ref[g, h, :, 3 * half : 3 * half + LANES].astype(F32),
                )
            )
    both_sweeps(order_ref, tails, movie_ref, turned_ref, own_ref, other_ref, final_ref)
    pick(final_ref, idx_ref, out_ref, odd * side, side // LANES, start_ref)


def local(sizes, movie, traces, voxel_index, footprint, block_order):
    frames, slabs = sizes
    both = ("frames", "slabs")
    rows, voxels = movie.shape
    half = voxels // 2
    sources = traces.shape[1]
    side = voxels
    slab = lax.axis_index("slabs").astype(jnp.int32)
    odd = lax.rem(slab, 2)
    live = jnp.where((slab == 0) | (slab == slabs - 1), 0, 1).astype(jnp.int32)
    where = jnp.stack([odd, lax.axis_index("frames").astype(jnp.int32), live])
    wide = half + LANES + 4 * (side // 8)
    out, own_far, own_near = call(
        front_kernel,
        [jax.ShapeDtypeStruct((FAR, rows, wide), BF16)] + [jax.ShapeDtypeStruct((sources, side), F32)] * 2,
        [where], [voxel_index, footprint, movie, traces],
        [pltpu.VMEM((sources * 2 * side // LANES, LANES), F32)], limit=60,
    )
    got = lax.all_to_all(
        out, both, 0, 0,
        axis_index_groups=[
            [f * slabs + s % slabs for s in (a, a + 1) for f in (low, low + FAR)]
            for low in range(FAR) for a in range(1, slabs + 1, 2)
        ],
    )
    on_chip = [(f * slabs + s, f * slabs + (s ^ 1)) for f in range(frames) for s in range(slabs)]
    sent = call(middle_kernel, jax.ShapeDtypeStruct((FAR, 2, rows, wide + 2 * half), BF16), [where], [got])
    data = lax.all_to_all(
        sent, "frames", 0, 0,
        axis_index_groups=[list(range(a, a + FAR)) for a in range(0, frames, FAR)],
    )
    halo = lax.ppermute(
        call(
            near_kernel, jax.ShapeDtypeStruct((FAR, 2, rows, half + LANES + side // FAR), F32), [],
            [data, own_near],
        ),
        both, on_chip,
    )
    scratch = [pltpu.VMEM((frames * rows, side), F32), pltpu.VMEM((LANES, frames * rows), F32)]
    dense = pltpu.VMEM((sources, side), F32)
    result = jax.ShapeDtypeStruct(voxel_index.shape, F32)
    part = call(far_kernel, result, [where, block_order], [data, own_far, voxel_index], scratch + [dense, dense])
    return call(
        near_side_kernel, result, [where, block_order],
        [data, halo, own_near, voxel_index, part], scratch + [dense, dense],
    )


def solution(mesh):
    sizes = (mesh.shape["frames"], mesh.shape["slabs"])
    in_specs = (P("frames", "slabs"), P("frames", "slabs"), P("slabs", None), P("slabs", None), P())
    return jax.shard_map(
        functools.partial(local, sizes), mesh=mesh, in_specs=in_specs,
        out_specs=P("slabs", None), check_vma=False,
    )
```

time: 712 us -> 59.5 us (0.08)
  local copies, waits for them, and re-layouts: 505 us -> 0.02 us
  waiting for transfers between devices: 105 us -> 0.01 us
  starting transfers between devices: 50.6 us -> 2.04 us
  blocking collectives: 25.6 us -> 46.2 us
  between operations: 13.7 us -> 0.05 us
  Pallas kernels: 0 us -> 10.3 us
    gather x3 -> x0, local copies, waits for them, and re-layouts: 260 us -> none  [the longest x2 259 us: local(): return dense[rows, voxel_index]]
    unnamed x22 -> x10, local copies, waits for them, and re-layouts: 242 us -> 0.02 us
    psum x1 -> x0, waiting for transfers between devices: 91.7 us -> none  [local(): stat, gram = lax.psum((stat_part, gram_part), 'frames')]
    ppermute x8 -> x1, starting transfers between devices: 50.6 us -> 2.04 us  [local(): lax.ppermute(call(near_kernel, jax.ShapeDtypeStruct((FAR, 2, rows, half +...]
    all_to_all x0 -> x2, blocking collectives: none -> 46.2 us  [the longest x1 31.8 us: local(): lax.all_to_all(out, both, 0, 0, axis_index_groups=[[f * slabs + s % slabs...]
    psum x1 -> x0, blocking collectives: 25.6 us -> none  [local(): stat, gram = lax.psum((stat_part, gram_part), 'frames')]
    ppermute x8 -> x1, waiting for transfers between devices: 13 us -> 0.01 us  [local(): lax.ppermute(call(near_kernel, jax.ShapeDtypeStruct((FAR, 2, rows, half +...]
    pallas_call x0 -> x5, Pallas kernels: none -> 10.3 us  [call(): pl.pallas_call(body, out_shape=out_shape, in_specs=[smem] * len(scalars)...]
  transfers between devices with their start and end apart: 9 -> 1, of which waited for: 3 -> 0; matrix products, arithmetic and copies ran while one was open for 34% -> 0% of each run, Pallas kernels for 0% -> 4%
where the time goes in v2:
time: 59.5 us; the launch traced here: 59.2 us
  blocking collectives  46.2 us (78%)
  Pallas kernels  10.3 us (17%)
  starting transfers between devices  2.04 us (3%)
  other arithmetic  0.65 us (1%)
    all_to_all x1, blocking collectives, local(): lax.all_to_all(out, both, 0, 0, axis_index_groups=[[f * slabs + s % slabs...  31.8 us
    all_to_all x1, blocking collectives, local(): lax.all_to_all(sent, 'frames', 0, 0, axis_index_groups=[list(range(a, a +...  14.4 us
    pallas_call x5, Pallas kernels, call(): pl.pallas_call(body, out_shape=out_shape, in_specs=[smem] * len(scalars)...  10.3 us
    ppermute x1, starting transfers between devices, local(): lax.ppermute(call(near_kernel, jax.ShapeDtypeStruct((FAR, 2, rows, half +...  2.04 us
  transfers between devices with their start and end apart: 1, of which 0 were waited for; matrix products, arithmetic and copies ran while one was open for 0% of the time, Pallas kernels for 4%

profile of v2, /device:TPU:1, one launch (start us, length us, event | category | flops | bytes accessed | tf_op | source)
XLA Modules:
  0.0 59.2 jit_solution(12009126544141772713)
XLA Ops:
  0.0 0.7 %pad_add_fusion.where_ref = s32[3]{0:T(128)} fusion(s32[1]{0:T(128)} %bitcast.2, s32[1]{0:T(128)} %bitcast.1, s32[1]{0:T(128)} %bitcast), kind=kLoop, calls=%fused_computation | loop fusion | flops 6 | bytes 24 | tf_op jit(solution)/shard_map/stack | solution.py:261
  0.7 4.5 %shard_map.55 = (bf16[4,8,2176]{2,1,0:T(8,128)(2,1)}, f32[16,2048]{1,0:T(8,128)}, f32[16,2048]{1,0:T(8,128)}) custom-call(s32[3]{0:T(128)} %pad_add_fusion.where_ref, s32[16,2048]{1,0:T(8,128)} %idx_ref.5, f32[16,2048]{1,0:T(8,128)} %val_ref.1, bf16[8,2048]{1,0:T(8,128)(2,1)} %movie_ref.1, bf16[8,16]{1,0:T(8,128)(2,1)} %traces_ref.1), custom_call_target="tpu_custom_call" | custom-call | tf_op jit(solution)/shard_map/pallas_call | solution.py:20
  5.1 0.0 copy-start.3
  5.1 31.8 %all_to_all.10.in_ref = bf16[4,8,2176]{2,1,0:T(8,128)(2,1)S(1)} all-to-all(bf16[4,8,2176]{2,1,0:T(8,128)(2,1)} %get-tuple-element.8), channel_id=1, replica_groups={{1,257,2,258},{3,259,4,260},{5,261,6,262},{7,263,8,264},{9,265,10,266},..., dimensions={0} | all-to-all | bytes 278528 | tf_op jit(solution)/shard_map/all_to_all | solution.py:269
  36.9 0.0 copy-done.3
  36.9 0.6 %shard_map.56 = bf16[4,2,8,4224]{3,2,1,0:T(8,128)(2,1)S(1)} custom-call(s32[3]{0:T(128)S(1)} %copy-done.3, bf16[4,8,2176]{2,1,0:T(8,128)(2,1)S(1)} %all_to_all.10.in_ref), custom_call_target="tpu_custom_call" | custom-call | tf_op jit(solution)/shard_map/pallas_call | solution.py:20
  37.6 0.0 copy-start.1
  37.6 14.4 %all_to_all.11.data_ref = bf16[4,2,8,4224]{3,2,1,0:T(8,128)(2,1)S(1)} all-to-all(bf16[4,2,8,4224]{3,2,1,0:T(8,128)(2,1)S(1)} %shard_map.56), channel_id=1, replica_groups={{0,64,128,192},{256,320,384,448},{1,65,129,193},{257,321,385,449},{2,66..., dimensions={0} | all-to-all | bytes 1081344 | tf_op jit(solution)/shard_map/all_to_all | solution.py:278
  51.9 0.0 copy-done.1
  51.9 0.0 copy-start
  51.9 0.0 copy-start.2
  51.9 0.1 shard_map.57
  52.0 0.0 copy-start.4
  52.0 2.0 %collective-permute-start = (f32[4,2,8,1664]{3,2,1,0:T(8,128)S(1)}, f32[4,2,8,1664]{3,2,1,0:T(8,128)S(1)}, u32[]{:S(2)}, u32[]{:S(2)}) collective-permute-start(f32[4,2,8,1664]{3,2,1,0:T(8,128)S(1)} %shard_map.57), channel_id=1, source_target_pairs={{0,1},{1,0},{2,3},{3,2},{4,5},{5,4},{6,7},{7,6},{8,9},{9,8},{10,11... | collective-permute-start | bytes 1277960 | tf_op jit(solution)/shard_map/ppermute | solution.py:282
  54.1 0.0 copy-done
  54.1 0.0 copy-done.2
  54.1 0.0 copy-done.4
  54.1 2.2 %shard_map.58.start_ref = f32[16,2048]{1,0:T(8,128)S(1)} custom-call(s32[3]{0:T(128)S(1)} %copy-done.3, s32[2]{0:T(128)S(1)} %copy-done.4, bf16[4,2,8,4224]{3,2,1,0:T(8,128)(2,1)S(1)} %all_to_all.11.data_ref, f32[16,2048]{1,0:T(8,128)S(1)} %copy-done.2, s32[16,2048]{1,0:T(8,128)S(1)} %copy-done), custom_call_target="tpu_custom_call" | custom-call | tf_op jit(solution)/shard_map/pallas_call | solution.py:20
  56.3 0.0 collective-permute-done.halo_ref
  56.3 2.9 %shard_map.59 = f32[16,2048]{1,0:T(8,128)} custom-call(s32[3]{0:T(128)S(1)} %copy-done.3, s32[2]{0:T(128)S(1)} %copy-done.4, bf16[4,2,8,4224]{3,2,1,0:T(8,128)(2,1)S(1)} %all_to_all.11.data_ref, f32[4,2,8,1664]{3,2,1,0:T(8,128)S(1)} %collective-permute-done.halo_ref, f32[16,2048]{1,0:T(8,128)S(1)} %copy-done.1, s32[16,2048]{1,0:T(8,128)S(1)} %copy-done, ...), custom_call_target="tpu_custom_call" | custom-call | tf_op jit(solution)/shard_map/pallas_call | solution.py:20
Async XLA Ops:
  5.1 31.8 %copy-start.3 = (s32[3]{0:T(128)S(1)}, s32[3]{0:T(128)}, u32[]{:S(2)}) copy-start(s32[3]{0:T(128)} %pad_add_fusion.where_ref) | copy-start | bytes 40
  37.6 14.4 %copy-start.1 = (f32[16,2048]{1,0:T(8,128)S(1)}, f32[16,2048]{1,0:T(8,128)}, u32[]{:S(2)}) copy-start(f32[16,2048]{1,0:T(8,128)} %get-tuple-element.9.dense_ref.own_ref) | copy-start | bytes 393220
  51.9 2.1 %copy-start = (s32[16,2048]{1,0:T(8,128)S(1)}, s32[16,2048]{1,0:T(8,128)}, u32[]{:S(2)}) copy-start(s32[16,2048]{1,0:T(8,128)} %idx_ref.5) | copy-start | bytes 393220
  51.9 2.1 %copy-start.2 = (f32[16,2048]{1,0:T(8,128)S(1)}, f32[16,2048]{1,0:T(8,128)}, u32[]{:S(2)}) copy-start(f32[16,2048]{1,0:T(8,128)} %get-tuple-element.10.own_ref) | copy-start | bytes 393220
  52.0 2.1 %copy-start.4 = (s32[2]{0:T(128)S(1)}, s32[2]{0:T(128)}, u32[]{:S(2)}) copy-start(s32[2]{0:T(128)} %order_ref.3) | copy-start | bytes 28
  52.0 4.3 %collective-permute-start = (f32[4,2,8,1664]{3,2,1,0:T(8,128)S(1)}, f32[4,2,8,1664]{3,2,1,0:T(8,128)S(1)}, u32[]{:S(2)}, u32[]{:S(2)}) collective-permute-start(f32[4,2,8,1664]{3,2,1,0:T(8,128)S(1)} %shard_map.57), channel_id=1, source_target_pairs={{0,1},{1,0},{2,3},{3,2},{4,5},{5,4},{6,7},{7,6},{8,9},{9,8},{10,11... | collective-permute-start | bytes 1277960 | tf_op jit(solution)/shard_map/ppermute | solution.py:282

commit v3 on v2

--- a/solution.py
+++ b/solution.py
@@ -27,6 +27,13 @@
     )(*scalars, *arrays)
 
 
+def place():
+    slab = lax.axis_index("slabs")
+    last = lax.axis_size("slabs") - 1
+    live = jnp.where((slab == 0) | (slab == last), 0, 1)
+    return lax.rem(slab, 2), lax.axis_index("frames"), live
+
+
 def thirds(x):
     top = x.astype(BF16).astype(F32)
     rest = x - top
@@ -34,20 +41,21 @@
     return top, mid, rest - mid
 
 
-def front_kernel(where_ref, idx_ref, val_ref, movie_ref, traces_ref, out_ref, far_ref, near_ref, rows_ref):
+def front_kernel(idx_ref, val_ref, movie_ref, traces_ref, out_ref, far_ref, near_ref, rows_ref):
     sources, count = idx_ref.shape
     tiles = 2 * far_ref.shape[1] // LANES
-    odd, frame = where_ref[0], where_ref[1]
-    tile_ids = lax.broadcasted_iota(jnp.int32, (tiles, count), 0)
-    lane_ids = lax.broadcasted_iota(jnp.int32, (LANES, count), 0)
+    odd, frame, _ = place()
+    tile_ids = lax.broadcasted_iota(jnp.int32, (tiles, count), 0).astype(F32).astype(BF16)
+    lane_ids = lax.broadcasted_iota(jnp.int32, (LANES, count), 0).astype(F32).astype(BF16)
+    one, none = jnp.ones((1, 1), BF16), jnp.zeros((1, 1), BF16)
     for k in range(sources):
         pos = idx_ref[k : k + 1, :]
         val = val_ref[k : k + 1, :]
-        in_tile = tile_ids == (pos >> 7)
-        on_lane = (lane_ids == (pos & (LANES - 1))).astype(F32).astype(BF16)
+        in_tile = tile_ids == (pos >> 7).astype(F32).astype(BF16)
+        on_lane = jnp.where(lane_ids == (pos & (LANES - 1)).astype(F32).astype(BF16), one, none)
         left = jnp.concatenate(
-            [jnp.where(in_tile, part, 0.0) for part in thirds(val) + (jnp.ones_like(val),)], axis=0
-        ).astype(BF16)
+            [jnp.where(in_tile, part.astype(BF16), none) for part in thirds(val) + (jnp.ones_like(val),)], axis=0
+        )
         found = lax.dot_general(left, on_lane, (((1,), (1,)), ((), ())), preferred_element_type=F32)
         value = found[:tiles] + (found[tiles : 2 * tiles] + found[2 * tiles : 3 * tiles])
         rows_ref[k * tiles : (k + 1) * tiles, :] = jnp.where(found[3 * tiles :] > 0.5, value, -1.0)
@@ -79,10 +87,10 @@
             out_ref[2 - mine + h, :, pl.ds(half + LANES + i * share, share)] = part
 
 
-def middle_kernel(where_ref, in_ref, out_ref):
+def middle_kernel(in_ref, out_ref):
     rows = in_ref.shape[1]
     half = (out_ref.shape[3] - in_ref.shape[2]) // 2
-    odd, live = where_ref[0], where_ref[2]
+    odd, _, live = place()
     mine = 2 * (1 - odd)
     lane = lax.broadcasted_iota(jnp.int32, (rows, LANES), 1)
     for h in range(2):
@@ -193,13 +201,13 @@
             out_ref[r : r + BLOCK, c : c + LANES] = got
 
 
-def far_kernel(where_ref, order_ref, data_ref, own_ref, idx_ref, out_ref,
+def far_kernel(order_ref, data_ref, own_ref, idx_ref, out_ref,
                movie_ref, turned_ref, other_ref, final_ref):
     groups, pairs, rows, _ = data_ref.shape
     sources, side = own_ref.shape
     half = side // 2
     share = side // 8
-    odd = where_ref[0]
+    odd, _, _ = place()
     halo_cols = pl.ds(pl.multiple_of(odd * half, half), half)
     own_cols = pl.ds(pl.multiple_of(half - odd * half, half), half)
     tails = []
@@ -220,12 +228,12 @@
     pick(final_ref, idx_ref, out_ref, odd * side, 0, None)
 
 
-def near_side_kernel(where_ref, order_ref, data_ref, halo_ref, own_ref, idx_ref, start_ref, out_ref,
+def near_side_kernel(order_ref, data_ref, halo_ref, own_ref, idx_ref, start_ref, out_ref,
                      movie_ref, turned_ref, final_ref, other_ref):
     groups, pairs, rows, _ = data_ref.shape
     sources, side = own_ref.shape
     half = side // 2
-    odd = where_ref[0]
+    odd, _, _ = place()
     own_cols = pl.ds(pl.multiple_of(odd * half, half), half)
     halo_cols = pl.ds(pl.multiple_of(half - odd * half, half), half)
     lane = lax.broadcasted_iota(jnp.int32, (rows, LANES), 1)
@@ -255,15 +263,11 @@
     half = voxels // 2
     sources = traces.shape[1]
     side = voxels
-    slab = lax.axis_index("slabs").astype(jnp.int32)
-    odd = lax.rem(slab, 2)
-    live = jnp.where((slab == 0) | (slab == slabs - 1), 0, 1).astype(jnp.int32)
-    where = jnp.stack([odd, lax.axis_index("frames").astype(jnp.int32), live])
     wide = half + LANES + 4 * (side // 8)
     out, own_far, own_near = call(
         front_kernel,
         [jax.ShapeDtypeStruct((FAR, rows, wide), BF16)] + [jax.ShapeDtypeStruct((sources, side), F32)] * 2,
-        [where], [voxel_index, footprint, movie, traces],
+        [], [voxel_index, footprint, movie, traces],
         [pltpu.VMEM((sources * 2 * side // LANES, LANES), F32)], limit=60,
     )
     got = lax.all_to_all(
@@ -274,7 +278,7 @@
         ],
     )
     on_chip = [(f * slabs + s, f * slabs + (s ^ 1)) for f in range(frames) for s in range(slabs)]
-    sent = call(middle_kernel, jax.ShapeDtypeStruct((FAR, 2, rows, wide + 2 * half), BF16), [where], [got])
+    sent = call(middle_kernel, jax.ShapeDtypeStruct((FAR, 2, rows, wide + 2 * half), BF16), [], [got])
     data = lax.all_to_all(
         sent, "frames", 0, 0,
         axis_index_groups=[list(range(a, a + FAR)) for a in range(0, frames, FAR)],
@@ -289,9 +293,9 @@
     scratch = [pltpu.VMEM((frames * rows, side), F32), pltpu.VMEM((LANES, frames * rows), F32)]
     dense = pltpu.VMEM((sources, side), F32)
     result = jax.ShapeDtypeStruct(voxel_index.shape, F32)
-    part = call(far_kernel, result, [where, block_order], [data, own_far, voxel_index], scratch + [dense, dense])
+    part = call(far_kernel, result, [block_order], [data, own_far, voxel_index], scratch + [dense, dense])
     return call(
-        near_side_kernel, result, [where, block_order],
+        near_side_kernel, result, [block_order],
         [data, halo, own_near, voxel_index, part], scratch + [dense, dense],
     )
 

time: 59.5 us -> 57.8 us (0.971)
  Pallas kernels: 10.3 us -> 9.39 us
  other arithmetic: 0.65 us -> 0 us
    pallas_call x5, Pallas kernels: 10.3 us -> 9.39 us  [call(): pl.pallas_call(body, out_shape=out_shape, in_specs=[smem] * len(scalars)...]
    another operation x1 -> x0, other arithmetic: 0.65 us -> none  [local(): where = jnp.stack([odd, lax.axis_index('frames').astype(jnp.int32), live])]
where the time goes in v3:
time: 57.8 us; the launch traced here: 57.5 us
  blocking collectives  46 us (80%)
  Pallas kernels  9.39 us (16%)
  starting transfers between devices  2.04 us (4%)
    all_to_all x1, blocking collectives, local(): lax.all_to_all(out, both, 0, 0, axis_index_groups=[[f * slabs + s % slabs...  31.7 us
    all_to_all x1, blocking collectives, local(): lax.all_to_all(sent, 'frames', 0, 0, axis_index_groups=[list(range(a, a +...  14.4 us
    pallas_call x5, Pallas kernels, call(): pl.pallas_call(body, out_shape=out_shape, in_specs=[smem] * len(scalars)...  9.39 us
    ppermute x1, starting transfers between devices, local(): lax.ppermute(call(near_kernel, jax.ShapeDtypeStruct((FAR, 2, rows, half +...  2.04 us
  transfers between devices with their start and end apart: 1, of which 0 were waited for; matrix products, arithmetic and copies ran while one was open for 0% of the time, Pallas kernels for 4%

profile of v3, /device:TPU:1, one launch (start us, length us, event | category | flops | bytes accessed | tf_op | source)
XLA Modules:
  0.0 57.5 jit_solution(17455250928155401720)
XLA Ops:
  0.0 4.1 %shard_map.55 = (bf16[4,8,2176]{2,1,0:T(8,128)(2,1)}, f32[16,2048]{1,0:T(8,128)}, f32[16,2048]{1,0:T(8,128)}) custom-call(s32[16,2048]{1,0:T(8,128)} %idx_ref.5, f32[16,2048]{1,0:T(8,128)} %val_ref.1, bf16[8,2048]{1,0:T(8,128)(2,1)} %movie_ref.1, bf16[8,16]{1,0:T(8,128)(2,1)} %traces_ref.1), custom_call_target="tpu_custom_call" | custom-call | tf_op jit(solution)/shard_map/pallas_call | solution.py:20
  4.1 31.7 %all_to_all.10.in_ref = bf16[4,8,2176]{2,1,0:T(8,128)(2,1)S(1)} all-to-all(bf16[4,8,2176]{2,1,0:T(8,128)(2,1)} %get-tuple-element.8), channel_id=1, replica_groups={{1,257,2,258},{3,259,4,260},{5,261,6,262},{7,263,8,264},{9,265,10,266},..., dimensions={0} | all-to-all | bytes 278528 | tf_op jit(solution)/shard_map/all_to_all | solution.py:273
  35.8 0.1 shard_map.56
  35.9 0.0 copy-start.1
  35.9 14.4 %all_to_all.11.data_ref = bf16[4,2,8,4224]{3,2,1,0:T(8,128)(2,1)S(1)} all-to-all(bf16[4,2,8,4224]{3,2,1,0:T(8,128)(2,1)S(1)} %shard_map.56), channel_id=1, replica_groups={{0,64,128,192},{256,320,384,448},{1,65,129,193},{257,321,385,449},{2,66..., dimensions={0} | all-to-all | bytes 1081344 | tf_op jit(solution)/shard_map/all_to_all | solution.py:282
  50.2 0.0 copy-done.1
  50.2 0.0 copy-start
  50.2 0.0 copy-start.2
  50.2 0.1 shard_map.57
  50.3 0.0 copy-start.3
  50.3 2.0 %collective-permute-start = (f32[4,2,8,1664]{3,2,1,0:T(8,128)S(1)}, f32[4,2,8,1664]{3,2,1,0:T(8,128)S(1)}, u32[]{:S(2)}, u32[]{:S(2)}) collective-permute-start(f32[4,2,8,1664]{3,2,1,0:T(8,128)S(1)} %shard_map.57), channel_id=1, source_target_pairs={{0,1},{1,0},{2,3},{3,2},{4,5},{5,4},{6,7},{7,6},{8,9},{9,8},{10,11... | collective-permute-start | bytes 1277960 | tf_op jit(solution)/shard_map/ppermute | solution.py:286
  52.4 0.0 copy-done
  52.4 0.0 copy-done.2
  52.4 0.0 copy-done.3
  52.4 2.2 %shard_map.58.start_ref = f32[16,2048]{1,0:T(8,128)S(1)} custom-call(s32[2]{0:T(128)S(1)} %copy-done.3, bf16[4,2,8,4224]{3,2,1,0:T(8,128)(2,1)S(1)} %all_to_all.11.data_ref, f32[16,2048]{1,0:T(8,128)S(1)} %copy-done.2, s32[16,2048]{1,0:T(8,128)S(1)} %copy-done), custom_call_target="tpu_custom_call" | custom-call | tf_op jit(solution)/shard_map/pallas_call | solution.py:20
  54.6 0.0 collective-permute-done.halo_ref
  54.6 2.9 %shard_map.59 = f32[16,2048]{1,0:T(8,128)} custom-call(s32[2]{0:T(128)S(1)} %copy-done.3, bf16[4,2,8,4224]{3,2,1,0:T(8,128)(2,1)S(1)} %all_to_all.11.data_ref, f32[4,2,8,1664]{3,2,1,0:T(8,128)S(1)} %collective-permute-done.halo_ref, f32[16,2048]{1,0:T(8,128)S(1)} %copy-done.1, s32[16,2048]{1,0:T(8,128)S(1)} %copy-done, f32[16,2048]{1,0:T(8,128)S(1)} %shard_map.58.start_ref), custom_call_target="tpu_custom_call" | custom-call | tf_op jit(solution)/shard_map/pallas_call | solution.py:20
Async XLA Ops:
  35.9 14.4 %copy-start.1 = (f32[16,2048]{1,0:T(8,128)S(1)}, f32[16,2048]{1,0:T(8,128)}, u32[]{:S(2)}) copy-start(f32[16,2048]{1,0:T(8,128)} %get-tuple-element.9.dense_ref.own_ref) | copy-start | bytes 393220
  50.2 2.1 %copy-start = (s32[16,2048]{1,0:T(8,128)S(1)}, s32[16,2048]{1,0:T(8,128)}, u32[]{:S(2)}) copy-start(s32[16,2048]{1,0:T(8,128)} %idx_ref.5) | copy-start | bytes 393220
  50.2 2.1 %copy-start.2 = (f32[16,2048]{1,0:T(8,128)S(1)}, f32[16,2048]{1,0:T(8,128)}, u32[]{:S(2)}) copy-start(f32[16,2048]{1,0:T(8,128)} %get-tuple-element.10.own_ref) | copy-start | bytes 393220
  50.3 2.1 %copy-start.3 = (s32[2]{0:T(128)S(1)}, s32[2]{0:T(128)}, u32[]{:S(2)}) copy-start(s32[2]{0:T(128)} %order_ref.3) | copy-start | bytes 28
  50.3 4.3 %collective-permute-start = (f32[4,2,8,1664]{3,2,1,0:T(8,128)S(1)}, f32[4,2,8,1664]{3,2,1,0:T(8,128)S(1)}, u32[]{:S(2)}, u32[]{:S(2)}) collective-permute-start(f32[4,2,8,1664]{3,2,1,0:T(8,128)S(1)} %shard_map.57), channel_id=1, source_target_pairs={{0,1},{1,0},{2,3},{3,2},{4,5},{5,4},{6,7},{7,6},{8,9},{9,8},{10,11... | collective-permute-start | bytes 1277960 | tf_op jit(solution)/shard_map/ppermute | solution.py:286

commit v4 on v3

--- a/solution.py
+++ b/solution.py
@@ -12,6 +12,7 @@
 BLOCK = 8
 LANES = 128
 FAR = 4
+CROSS = 2
 
 
 def call(body, out_shape, scalars, arrays, scratch=(), limit=16):
@@ -210,14 +211,21 @@
     odd, _, _ = place()
     halo_cols = pl.ds(pl.multiple_of(odd * half, half), half)
     own_cols = pl.ds(pl.multiple_of(half - odd * half, half), half)
+    lane = lax.broadcasted_iota(jnp.int32, (rows, LANES), 1)
     tails = []
     for g in range(groups):
         for h in range(pairs):
             at = pl.ds((g * pairs + h) * rows, rows)
-            movie_ref[at, halo_cols] = data_ref[g, h, :, :half].astype(F32)
+            far = g ^ CROSS
+            movie_ref[at, halo_cols] = data_ref[far, h, :, :half].astype(F32)
             movie_ref[at, own_cols] = data_ref[g, h, :, half : 2 * half].astype(F32)
-            tails.append(data_ref[g, h, :, 3 * half : 3 * half + LANES].astype(F32))
-            frame = g + FAR * h
+            tail = pl.ds(3 * half, LANES)
+            tails.append(
+                jnp.where(
+                    lane < sources, data_ref[far, h, :, tail].astype(F32), data_ref[g, h, :, tail].astype(F32)
+                )
+            )
+            frame = far + FAR * h
             for i in range(sources // rows):
                 top, low = [
                     data_ref[g, h, :, pl.ds(3 * half + LANES + (n * (sources // rows) + i) * share, share)].astype(F32)
@@ -273,7 +281,7 @@
     got = lax.all_to_all(
         out, both, 0, 0,
         axis_index_groups=[
-            [f * slabs + s % slabs for s in (a, a + 1) for f in (low, low + FAR)]
+            [f * slabs + s % slabs for s, at in ((a, low), (a + 1, low ^ CROSS)) for f in (at, at + FAR)]
             for low in range(FAR) for a in range(1, slabs + 1, 2)
         ],
     )

time: 57.8 us -> 57.6 us (level)
  blocking collectives: 46 us -> 44.6 us
  starting transfers between devices: 2.04 us -> 3.28 us
    all_to_all x1, blocking collectives: 31.7 us -> 27 us  [local(): lax.all_to_all(out, both, 0, 0, axis_index_groups=[[f * slabs + s % slabs...]
    all_to_all x1, blocking collectives: 14.4 us -> 17.6 us  [local(): lax.all_to_all(sent, 'frames', 0, 0, axis_index_groups=[list(range(a, a +...]
    ppermute x1, starting transfers between devices: 2.04 us -> 3.28 us  [local(): lax.ppermute(call(near_kernel, jax.ShapeDtypeStruct((FAR, 2, rows, half +...]
where the time goes in v4:
time: 57.6 us; the launch traced here: 57.3 us
  blocking collectives  44.6 us (77%)
  Pallas kernels  9.4 us (16%)
  starting transfers between devices  3.28 us (6%)
    all_to_all x1, blocking collectives, local(): lax.all_to_all(out, both, 0, 0, axis_index_groups=[[f * slabs + s % slabs...  27 us
    all_to_all x1, blocking collectives, local(): lax.all_to_all(sent, 'frames', 0, 0, axis_index_groups=[list(range(a, a +...  17.6 us
    pallas_call x5, Pallas kernels, call(): pl.pallas_call(body, out_shape=out_shape, in_specs=[smem] * len(scalars)...  9.4 us
    ppermute x1, starting transfers between devices, local(): lax.ppermute(call(near_kernel, jax.ShapeDtypeStruct((FAR, 2, rows, half +...  3.28 us
  transfers between devices with their start and end apart: 1, of which 0 were waited for; matrix products, arithmetic and copies ran while one was open for 0% of the time, Pallas kernels for 4%

profile of v4, /device:TPU:1, one launch (start us, length us, event | category | flops | bytes accessed | tf_op | source)
XLA Modules:
  0.0 57.3 jit_solution(16789073307096661424)
XLA Ops:
  0.0 4.1 %shard_map.55 = (bf16[4,8,2176]{2,1,0:T(8,128)(2,1)}, f32[16,2048]{1,0:T(8,128)}, f32[16,2048]{1,0:T(8,128)}) custom-call(s32[16,2048]{1,0:T(8,128)} %idx_ref.5, f32[16,2048]{1,0:T(8,128)} %val_ref.1, bf16[8,2048]{1,0:T(8,128)(2,1)} %movie_ref.1, bf16[8,16]{1,0:T(8,128)(2,1)} %traces_ref.1), custom_call_target="tpu_custom_call" | custom-call | tf_op jit(solution)/shard_map/pallas_call | solution.py:21
  4.1 27.0 %all_to_all.10.in_ref = bf16[4,8,2176]{2,1,0:T(8,128)(2,1)S(1)} all-to-all(bf16[4,8,2176]{2,1,0:T(8,128)(2,1)} %get-tuple-element.8), channel_id=1, replica_groups={{1,257,130,386},{3,259,132,388},{5,261,134,390},{7,263,136,392},{9,265,..., dimensions={0} | all-to-all | bytes 278528 | tf_op jit(solution)/shard_map/all_to_all | solution.py:281
  31.1 0.1 shard_map.56
  31.2 0.0 copy-start.1
  31.2 17.6 %all_to_all.11.data_ref = bf16[4,2,8,4224]{3,2,1,0:T(8,128)(2,1)S(1)} all-to-all(bf16[4,2,8,4224]{3,2,1,0:T(8,128)(2,1)S(1)} %shard_map.56), channel_id=1, replica_groups={{0,64,128,192},{256,320,384,448},{1,65,129,193},{257,321,385,449},{2,66..., dimensions={0} | all-to-all | bytes 1081344 | tf_op jit(solution)/shard_map/all_to_all | solution.py:290
  48.8 0.0 copy-done.1
  48.8 0.0 copy-start
  48.8 0.0 copy-start.2
  48.8 0.1 shard_map.57
  48.9 0.0 copy-start.3
  48.9 3.3 %collective-permute-start = (f32[4,2,8,1664]{3,2,1,0:T(8,128)S(1)}, f32[4,2,8,1664]{3,2,1,0:T(8,128)S(1)}, u32[]{:S(2)}, u32[]{:S(2)}) collective-permute-start(f32[4,2,8,1664]{3,2,1,0:T(8,128)S(1)} %shard_map.57), channel_id=1, source_target_pairs={{0,1},{1,0},{2,3},{3,2},{4,5},{5,4},{6,7},{7,6},{8,9},{9,8},{10,11... | collective-permute-start | bytes 1277960 | tf_op jit(solution)/shard_map/ppermute | solution.py:294
  52.2 0.0 copy-done
  52.2 0.0 copy-done.2
  52.2 0.0 copy-done.3
  52.2 2.2 %shard_map.58.start_ref = f32[16,2048]{1,0:T(8,128)S(1)} custom-call(s32[2]{0:T(128)S(1)} %copy-done.3, bf16[4,2,8,4224]{3,2,1,0:T(8,128)(2,1)S(1)} %all_to_all.11.data_ref, f32[16,2048]{1,0:T(8,128)S(1)} %copy-done.2, s32[16,2048]{1,0:T(8,128)S(1)} %copy-done), custom_call_target="tpu_custom_call" | custom-call | tf_op jit(solution)/shard_map/pallas_call | solution.py:21
  54.4 0.0 collective-permute-done.halo_ref
  54.4 2.9 %shard_map.59 = f32[16,2048]{1,0:T(8,128)} custom-call(s32[2]{0:T(128)S(1)} %copy-done.3, bf16[4,2,8,4224]{3,2,1,0:T(8,128)(2,1)S(1)} %all_to_all.11.data_ref, f32[4,2,8,1664]{3,2,1,0:T(8,128)S(1)} %collective-permute-done.halo_ref, f32[16,2048]{1,0:T(8,128)S(1)} %copy-done.1, s32[16,2048]{1,0:T(8,128)S(1)} %copy-done, f32[16,2048]{1,0:T(8,128)S(1)} %shard_map.58.start_ref), custom_call_target="tpu_custom_call" | custom-call | tf_op jit(solution)/shard_map/pallas_call | solution.py:21
Async XLA Ops:
  31.2 17.6 %copy-start.1 = (f32[16,2048]{1,0:T(8,128)S(1)}, f32[16,2048]{1,0:T(8,128)}, u32[]{:S(2)}) copy-start(f32[16,2048]{1,0:T(8,128)} %get-tuple-element.9.dense_ref.own_ref) | copy-start | bytes 393220
  48.8 3.4 %copy-start = (s32[16,2048]{1,0:T(8,128)S(1)}, s32[16,2048]{1,0:T(8,128)}, u32[]{:S(2)}) copy-start(s32[16,2048]{1,0:T(8,128)} %idx_ref.5) | copy-start | bytes 393220
  48.8 3.4 %copy-start.2 = (f32[16,2048]{1,0:T(8,128)S(1)}, f32[16,2048]{1,0:T(8,128)}, u32[]{:S(2)}) copy-start(f32[16,2048]{1,0:T(8,128)} %get-tuple-element.10.own_ref) | copy-start | bytes 393220
  48.9 3.3 %copy-start.3 = (s32[2]{0:T(128)S(1)}, s32[2]{0:T(128)}, u32[]{:S(2)}) copy-start(s32[2]{0:T(128)} %order_ref.3) | copy-start | bytes 28
  48.9 5.6 %collective-permute-start = (f32[4,2,8,1664]{3,2,1,0:T(8,128)S(1)}, f32[4,2,8,1664]{3,2,1,0:T(8,128)S(1)}, u32[]{:S(2)}, u32[]{:S(2)}) collective-permute-start(f32[4,2,8,1664]{3,2,1,0:T(8,128)S(1)} %shard_map.57), channel_id=1, source_target_pairs={{0,1},{1,0},{2,3},{3,2},{4,5},{5,4},{6,7},{7,6},{8,9},{9,8},{10,11... | collective-permute-start | bytes 1277960 | tf_op jit(solution)/shard_map/ppermute | solution.py:294
